TPU v7x, 32 devices: a whole 2x2x4 slice. The times are simulated.
32 devices in a mesh: groups: 2 (over y), seq: 4 (over z), dp: 2 (over x), mp: 2 (over core).
Axes of the slice: x: 2, y: 2, z: 4, core: 2. Of those that a mesh axis runs over, the one named last changes fastest.
Arguments:
- queries: bfloat16 [4, 512, 2048], P(('groups', 'dp'), 'seq', 'mp'), parts along dimension 0, may hold values from -6 to 6
- keys: bfloat16 [4, 512, 2048], P(('groups', 'dp'), 'seq', 'mp'), parts along dimension 0, may hold values from -6 to 6
- values: bfloat16 [4, 512, 2048], P(('groups', 'dp'), 'seq', 'mp'), parts along dimension 0, may hold values from -6 to 6
- grad_output: bfloat16 [4, 512, 2048], P(('groups', 'dp'), 'seq', 'mp'), parts along dimension 0, may hold values from -6 to 6
- counts: int32 [4, 4, 4], P(('groups', 'dp'), 'seq'), parts along dimension 0, may hold values from 0 to 64, as said below
Outputs:
- grad_queries: bfloat16 [4, 512, 2048], P(('groups', 'dp'), 'seq', 'mp'), parts along dimension 0
- grad_keys: bfloat16 [4, 512, 2048], P(('groups', 'dp'), 'seq', 'mp'), parts along dimension 0
- grad_values: bfloat16 [4, 512, 2048], P(('groups', 'dp'), 'seq', 'mp'), parts along dimension 0
There are 2 independent parts, one for each index of `groups`. A program takes and returns all parts, laid end to end along the dimension named above; each array names one. Nothing has to cross between parts.
Inputs may be any that keep to these rules, and one draw needn't show every extreme that they name: Each shard's counts sum to 128; no entry exceeds 64, some window receives 64 points from every shard.
All inputs are finite; a program needn't handle non-finite values.
Results may differ from a plain program's by a relative error of at most 0.001.
Values may be sent and summed in bfloat16 or wider, within the bound.
A program may use at most 128 MiB of HBM per device.

v0:
```python
import math
import jax
import jax.numpy as jnp
from jax import lax
from jax.sharding import PartitionSpec as P

DH = 128
highest = lax.Precision.HIGHEST


def entering(value, axis, join, neutral, backward):
    count, mine = (lax.axis_size(axis), lax.axis_index(axis))
    pieces = lax.all_gather(value, axis)
    if backward:
        pieces = pieces[::-1]
        mine = count - 1 - mine
    total = jnp.full_like(value, 0) + jnp.asarray(neutral, value.dtype)

    def hop(position, total):
        longer = join(total, pieces[position])
        return jnp.where(position < mine, longer, total)

    return lax.fori_loop(0, count - 1, hop, total)


def add_states(earlier, later):
    return earlier + later


def per_device(queries, keys, values, grad_output, counts):
    shard_count = lax.axis_size("seq")
    local_rows = queries.shape[1]
    width = queries.shape[2]
    local_heads = width // DH
    capacity = 2 * local_rows // shard_count
    window_rows = shard_count * capacity
    factor = 1.0 / math.sqrt(DH * local_rows * shard_count)
    my_counts = counts[0, 0]
    window_ends = jnp.cumsum(my_counts)
    window_starts = window_ends - my_counts
    offsets = jnp.arange(capacity, dtype=jnp.int32)
    occupied = offsets[None, :] < my_counts[:, None]
    picked = jnp.where(occupied, window_starts[:, None] + offsets[None, :], 0).reshape(-1)
    occupied_column = occupied.reshape(-1, 1)

    def pack(source):
        taken = jnp.take(source[0], picked, axis=0)
        taken = jnp.where(occupied_column, taken, jnp.zeros_like(taken))
        return taken.reshape(shard_count, capacity, width)

    def split_heads(received):
        return received.reshape(window_rows, local_heads, DH)

    def outer_sum(left, right):
        return jnp.einsum("lha,lhb->hab", left, right, preferred_element_type=jnp.float32)

    query_recv, key_recv, value_recv, grad_recv = (
        lax.all_to_all(pack(queries), "seq", split_axis=0, concat_axis=0, tiled=True),
        lax.all_to_all(pack(keys), "seq", split_axis=0, concat_axis=0, tiled=True),
        lax.all_to_all(pack(values), "seq", split_axis=0, concat_axis=0, tiled=True),
        lax.all_to_all(pack(grad_output), "seq", split_axis=0, concat_axis=0, tiled=True),
    )
    query_recv = split_heads(query_recv)
    key_recv = split_heads(key_recv)
    value_recv = split_heads(value_recv)
    grad_recv = split_heads(grad_recv)
    key_state = outer_sum(key_recv, value_recv)
    query_state = outer_sum(query_recv, grad_recv)
    zero_state = jnp.zeros((local_heads, DH, DH), jnp.float32)
    before_kv = entering(key_state, "seq", add_states, zero_state, False)
    after_qd = entering(query_state, "seq", add_states, zero_state, True)
    block = min(512, window_rows)
    nblocks = window_rows // block

    def blocked(received):
        return received.reshape(nblocks, block, local_heads, DH)

    query_blocks = blocked(query_recv)
    key_blocks = blocked(key_recv)
    value_blocks = blocked(value_recv)
    grad_blocks = blocked(grad_recv)
    block_kv = jnp.einsum(
        "nlha,nlhb->nhab", key_blocks, value_blocks, preferred_element_type=jnp.float32
    )
    block_qd = jnp.einsum(
        "nlha,nlhb->nhab", query_blocks, grad_blocks, preferred_element_type=jnp.float32
    )
    kv_before = before_kv[None] + jnp.cumsum(block_kv, axis=0) - block_kv
    qd_after = after_qd[None] + jnp.sum(block_qd, axis=0)[None] - jnp.cumsum(block_qd, axis=0)
    lower = (
        lax.broadcasted_iota(jnp.int32, (block, block), 0)
        >= lax.broadcasted_iota(jnp.int32, (block, block), 1)
    ).astype(jnp.float32)

    def one_block(pieces):
        query_part, key_part, value_part, grad_part, kv_state, qd_state = pieces
        weights = (
            jnp.einsum("rha,sha->hrs", grad_part, value_part, preferred_element_type=jnp.float32)
            * lower[None]
        )
        scores = (
            jnp.einsum("rha,sha->hrs", query_part, key_part, preferred_element_type=jnp.float32)
            * lower[None]
        )
        query_f = query_part.astype(jnp.float32)
        key_f = key_part.astype(jnp.float32)
        value_f = value_part.astype(jnp.float32)
        grad_f = grad_part.astype(jnp.float32)
        grad_q = jnp.einsum("rhb,hab->rha", grad_f, kv_state, precision=highest) + jnp.einsum(
            "hrs,sha->rha", weights, key_f, precision=highest
        )
        grad_k = jnp.einsum("shb,hab->sha", value_f, qd_state, precision=highest) + jnp.einsum(
            "hrs,rha->sha", weights, query_f, precision=highest
        )
        grad_v = jnp.einsum("sha,hab->shb", key_f, qd_state, precision=highest) + jnp.einsum(
            "hrs,rhb->shb", scores, grad_f, precision=highest
        )

        def finish(result):
            return (result * factor).astype(jnp.bfloat16).reshape(block, width)

        return (finish(grad_q), finish(grad_k), finish(grad_v))

    out_q, out_k, out_v = lax.map(
        one_block, (query_blocks, key_blocks, value_blocks, grad_blocks, kv_before, qd_after)
    )

    def to_slots(result):
        return result.reshape(shard_count, capacity, width)

    back_q, back_k, back_v = (
        lax.all_to_all(to_slots(out_q), "seq", split_axis=0, concat_axis=0, tiled=True),
        lax.all_to_all(to_slots(out_k), "seq", split_axis=0, concat_axis=0, tiled=True),
        lax.all_to_all(to_slots(out_v), "seq", split_axis=0, concat_axis=0, tiled=True),
    )
    positions = jnp.arange(local_rows, dtype=jnp.int32)
    member = (
        (positions[:, None] >= window_starts[None, :]) & (positions[:, None] < window_ends[None, :])
    ).astype(jnp.int32)
    window_of = jnp.sum(member * jnp.arange(shard_count, dtype=jnp.int32)[None, :], axis=1)
    start_of = jnp.sum(member * window_starts[None, :], axis=1)
    source_index = window_of * capacity + positions - start_of

    def unpack(returned):
        return jnp.take(returned.reshape(window_rows, width), source_index, axis=0)[None]

    return (unpack(back_q), unpack(back_k), unpack(back_v))


def solution(mesh):
    placed = (
        P(("groups", "dp"), "seq", "mp"),
        P(("groups", "dp"), "seq", "mp"),
        P(("groups", "dp"), "seq", "mp"),
        P(("groups", "dp"), "seq", "mp"),
        P(("groups", "dp"), "seq", None),
    )
    return jax.shard_map(
        per_device,
        mesh=mesh,
        in_specs=placed,
        out_specs=(
            P(("groups", "dp"), "seq", "mp"),
            P(("groups", "dp"), "seq", "mp"),
            P(("groups", "dp"), "seq", "mp"),
        ),
        check_vma=False,
    )
```

profile of v0, /device:TPU:0, one launch (start us, length us, event | category | flops | bytes accessed | tf_op | source)
XLA Modules:
  0.0 218.9 jit_solution(3963657289021872831)
XLA Ops:
  15.8 20.6 %all_to_all.35 = bf16[4,64,1024]{2,1,0:T(8,128)(2,1)S(1)} all-to-all(bf16[4,64,1024]{2,1,0:T(8,128)(2,1)S(1)} %bitcast.68), channel_id=1, replica_groups=mesh['groups'=2,'seq'=4,'dp'=2,'mp'=2] {'seq'}, dimensions={0} | all-to-all | bytes 1048576 | tf_op jit(solution)/shard_map/all_to_all | solution.py:61
  36.4 3.5 %all-to-all-start.4 = ((bf16[4,64,1024]{2,1,0:T(8,128)(2,1)}), bf16[4,64,1024]{2,1,0:T(8,128)(2,1)S(1)}, u32[]{:S(2)}, u32[]{:S(2)}) async-start(bf16[4,64,1024]{2,1,0:T(8,128)(2,1)} %bitcast.14), calls=%async_computation.4 | async-start | bytes 1048576 | tf_op jit(solution)/shard_map/all_to_all | solution.py:58
  40.4 13.1 %all-to-all-done.4 = bf16[4,64,1024]{2,1,0:T(8,128)(2,1)S(1)} async-done(((bf16[4,64,1024]{2,1,0:T(8,128)(2,1)}), bf16[4,64,1024]{2,1,0:T(8,128)(2,1)S(1)}, u32[]{:S(2)}, u32[]{:S(2)}) %all-to-all-start.4) | async-done | bytes 524320 | tf_op jit(solution)/shard_map/all_to_all | solution.py:58
  54.8 27.9 %all_to_all.36 = bf16[4,64,1024]{2,1,0:T(8,128)(2,1)S(1)} all-to-all(bf16[4,64,1024]{2,1,0:T(8,128)(2,1)S(1)} %bitcast.67), channel_id=1, replica_groups=mesh['groups'=2,'seq'=4,'dp'=2,'mp'=2] {'seq'}, dimensions={0} | all-to-all | bytes 1048576 | tf_op jit(solution)/shard_map/all_to_all | solution.py:59
  82.7 4.1 %all-to-all-start.1 = ((bf16[4,64,1024]{2,1,0:T(8,128)(2,1)}), bf16[4,64,1024]{2,1,0:T(8,128)(2,1)S(1)}, u32[]{:S(2)}, u32[]{:S(2)}) async-start(bf16[4,64,1024]{2,1,0:T(8,128)(2,1)} %bitcast.6), calls=%async_computation.1 | async-start | bytes 1048576 | tf_op jit(solution)/shard_map/all_to_all | solution.py:60
  87.0 25.5 %all-to-all-done.1 = bf16[4,64,1024]{2,1,0:T(8,128)(2,1)S(1)} async-done(((bf16[4,64,1024]{2,1,0:T(8,128)(2,1)}), bf16[4,64,1024]{2,1,0:T(8,128)(2,1)S(1)}, u32[]{:S(2)}, u32[]{:S(2)}) %all-to-all-start.1) | async-done | bytes 524320 | tf_op jit(solution)/shard_map/all_to_all | solution.py:60
  113.3 2.2 fusion.55
  115.6 1.8 fusion.49
  117.4 3.2 %rev.3 = f32[4,8,128,128]{3,2,1,0:T(8,128)} reverse(f32[4,8,128,128]{3,2,1,0:T(8,128)} %bitcast.69), dimensions={0} | reverse | bytes 4194304 | tf_op jit(solution)/shard_map/rev | solution.py:15
  120.7 3.8 %while.35 = (s32[]{:T(128)}, f32[8,128,128]{2,1,0:T(8,128)S(1)}, s32[]{:T(128)}, f32[4,8,128,128]{3,2,1,0:T(8,128)}, s32[]{:T(128)}, /*index=5*/s32[]{:T(128)}) while((s32[]{:T(128)}, f32[8,128,128]{2,1,0:T(8,128)S(1)}, s32[]{:T(128)}, f32[4,8,128,128]{3,2,1,0:T(8,128)}, s32[]{:T(128)}, /*index=5*/s32[]{:T(128)}) %tuple.75), condition=%wide.region_6.9_spmd.clone, body=%wide.region_5.8_spmd.clone.sunk | while | flops 393220 | bytes 1572965 | solution.py:23
  128.6 4.1 %all-to-all-start.6 = ((bf16[4,64,1024]{2,1,0:T(8,128)(2,1)}), bf16[4,64,1024]{2,1,0:T(8,128)(2,1)}, u32[]{:S(2)}, u32[]{:S(2)}) async-start(bf16[4,64,1024]{2,1,0:T(8,128)(2,1)} %reshape.172), calls=%async_computation.6 | async-start | bytes 1048576 | tf_op jit(solution)/shard_map/all_to_all | solution.py:134
  132.7 1.8 fusion.53
  134.5 1.7 fusion.51
  138.5 2.1 reshape.170
  140.6 21.8 %all-to-all-done.6 = bf16[4,64,1024]{2,1,0:T(8,128)(2,1)} async-done(((bf16[4,64,1024]{2,1,0:T(8,128)(2,1)}), bf16[4,64,1024]{2,1,0:T(8,128)(2,1)}, u32[]{:S(2)}, u32[]{:S(2)}) %all-to-all-start.6) | async-done | bytes 524320 | tf_op jit(solution)/shard_map/all_to_all | solution.py:134
  162.4 4.3 %all-to-all-start.5 = ((bf16[4,64,1024]{2,1,0:T(8,128)(2,1)}), bf16[4,64,1024]{2,1,0:T(8,128)(2,1)}, u32[]{:S(2)}, u32[]{:S(2)}) async-start(bf16[4,64,1024]{2,1,0:T(8,128)(2,1)} %reshape.170), calls=%async_computation.5 | async-start | bytes 1048576 | tf_op jit(solution)/shard_map/all_to_all | solution.py:133
  166.7 17.4 %all-gather.5.cloned.1.call-done = f32[32,128,128]{2,1,0:T(8,128)} async-done(((f32[8,128,128]{2,1,0:T(8,128)}), f32[32,128,128]{2,1,0:T(8,128)}) %all-gather.5.cloned.1.call-update) | async-done | bytes 2097168 | tf_op jit(solution)/shard_map/all_gather | solution.py:13
  184.1 3.8 %while.34 = (s32[]{:T(128)}, f32[8,128,128]{2,1,0:T(8,128)S(1)}, s32[]{:T(128)}, f32[4,8,128,128]{3,2,1,0:T(8,128)}, s32[]{:T(128)}, /*index=5*/s32[]{:T(128)}) while((s32[]{:T(128)}, f32[8,128,128]{2,1,0:T(8,128)S(1)}, s32[]{:T(128)}, f32[4,8,128,128]{3,2,1,0:T(8,128)}, s32[]{:T(128)}, /*index=5*/s32[]{:T(128)}) %tuple.85), condition=%wide.region_2.4_spmd.clone, body=%wide.region_1.3_spmd.clone.sunk | while | flops 393220 | bytes 1572965 | solution.py:23
  187.9 1.7 fusion.45
  189.6 1.4 fusion.33
  192.5 3.5 %all-to-all-start.3 = ((bf16[4,64,1024]{2,1,0:T(8,128)(2,1)}), bf16[4,64,1024]{2,1,0:T(8,128)(2,1)S(1)}, u32[]{:S(2)}, u32[]{:S(2)}) async-start(bf16[4,64,1024]{2,1,0:T(8,128)(2,1)} %reshape.166), calls=%async_computation.3 | async-start | bytes 1048576 | tf_op jit(solution)/shard_map/all_to_all | solution.py:132
  196.0 2.2 gather_fusion.6
  198.2 2.2 gather_fusion.5
  200.4 9.9 %all-to-all-done.3 = bf16[4,64,1024]{2,1,0:T(8,128)(2,1)S(1)} async-done(((bf16[4,64,1024]{2,1,0:T(8,128)(2,1)}), bf16[4,64,1024]{2,1,0:T(8,128)(2,1)S(1)}, u32[]{:S(2)}, u32[]{:S(2)}) %all-to-all-start.3) | async-done | bytes 524320 | tf_op jit(solution)/shard_map/all_to_all | solution.py:132
  (79 shorter events, 28.5 us)
Async XLA Ops:
  7.2 2.5 %copy-start = (bf16[1,128,1024]{2,1,0:T(8,128)(2,1)S(1)}, bf16[1,128,1024]{2,1,0:T(8,128)(2,1)}, u32[]{:S(2)}) copy-start(bf16[1,128,1024]{2,1,0:T(8,128)(2,1)} %param.13) | copy-start | bytes 786436
  9.7 1.2 copy-start.1
  10.9 1.2 copy-start.2
  12.1 1.2 copy-start.3
  36.4 17.1 %all-to-all-start.4 = ((bf16[4,64,1024]{2,1,0:T(8,128)(2,1)}), bf16[4,64,1024]{2,1,0:T(8,128)(2,1)S(1)}, u32[]{:S(2)}, u32[]{:S(2)}) async-start(bf16[4,64,1024]{2,1,0:T(8,128)(2,1)} %bitcast.14), calls=%async_computation.4 | async-start | bytes 1048576 | tf_op jit(solution)/shard_map/all_to_all | solution.py:58
  39.9 77.6 %all-gather.7.cloned.1.call-start = ((), (), s32[]{:S(2)}) async-start(), calls=%async_computation.8 | async-start | bytes 2621440 | tf_op jit(solution)/shard_map/all_gather | solution.py:13
  40.3 84.8 %copy-start.4 = (bf16[256,8,128]{0,2,1:T(8,128)(2,1)}, bf16[256,8,128]{0,2,1:T(8,128)(2,1)S(1)}, u32[]{:S(2)}) copy-start(bf16[256,8,128]{0,2,1:T(8,128)(2,1)S(1)} %copy.66) | copy-start | bytes 1572868
  53.6 62.0 %copy-start.10 = (bf16[32,8,8,128]{3,2,1,0:T(8,128)(2,1)}, bf16[32,8,8,128]{3,2,1,0:T(8,128)(2,1)S(1)}, u32[]{:S(2)}) copy-start(bf16[32,8,8,128]{3,2,1,0:T(8,128)(2,1)S(1)} %copy.72) | copy-start | bytes 1572868
  82.7 29.7 %all-to-all-start.1 = ((bf16[4,64,1024]{2,1,0:T(8,128)(2,1)}), bf16[4,64,1024]{2,1,0:T(8,128)(2,1)S(1)}, u32[]{:S(2)}, u32[]{:S(2)}) async-start(bf16[4,64,1024]{2,1,0:T(8,128)(2,1)} %bitcast.6), calls=%async_computation.1 | async-start | bytes 1048576 | tf_op jit(solution)/shard_map/all_to_all | solution.py:60
  86.9 97.3 %all-gather.5.cloned.1.call-start = ((), (), s32[]{:S(2)}) async-start(), calls=%async_computation.7 | async-start | bytes 2621440 | tf_op jit(solution)/shard_map/all_gather | solution.py:13
  87.0 37.5 %copy-start.6 = (bf16[32,8,8,128]{3,2,1,0:T(8,128)(2,1)}, bf16[32,8,8,128]{3,2,1,0:T(8,128)(2,1)S(1)}, u32[]{:S(2)}) copy-start(bf16[32,8,8,128]{3,2,1,0:T(8,128)(2,1)S(1)} %copy.69) | copy-start | bytes 1572868
  115.6 9.5 %copy-start.13 = (f32[256,256]{1,0:T(8,128)}, f32[256,256]{1,0:T(8,128)S(1)}, u32[]{:S(2)}) copy-start(f32[256,256]{1,0:T(8,128)S(1)} %fusion.62) | copy-start | bytes 786436
  120.7 3.9 %copy-start.8 = (f32[8,128,128]{2,1,0:T(8,128)S(1)}, f32[8,128,128]{2,1,0:T(8,128)}, u32[]{:S(2)}) copy-start(f32[8,128,128]{2,1,0:T(8,128)} %fusion.47) | copy-start | bytes 1572868
  124.5 1.7 copy-start.12
  128.6 33.8 %all-to-all-start.6 = ((bf16[4,64,1024]{2,1,0:T(8,128)(2,1)}), bf16[4,64,1024]{2,1,0:T(8,128)(2,1)}, u32[]{:S(2)}, u32[]{:S(2)}) async-start(bf16[4,64,1024]{2,1,0:T(8,128)(2,1)} %reshape.172), calls=%async_computation.6 | async-start | bytes 1048576 | tf_op jit(solution)/shard_map/all_to_all | solution.py:134
  132.7 1.8 copy-start.9
  134.5 1.7 copy-start.11
  134.5 1.7 copy-start.14
  162.4 30.1 %all-to-all-start.5 = ((bf16[4,64,1024]{2,1,0:T(8,128)(2,1)}), bf16[4,64,1024]{2,1,0:T(8,128)(2,1)}, u32[]{:S(2)}, u32[]{:S(2)}) async-start(bf16[4,64,1024]{2,1,0:T(8,128)(2,1)} %reshape.170), calls=%async_computation.5 | async-start | bytes 1048576 | tf_op jit(solution)/shard_map/all_to_all | solution.py:133
  184.1 3.8 %copy-start.5 = (bf16[256,8,128]{0,2,1:T(8,128)(2,1)S(1)}, bf16[256,8,128]{0,2,1:T(8,128)(2,1)}, u32[]{:S(2)}) copy-start(bf16[256,8,128]{0,2,1:T(8,128)(2,1)} %copy-done.4) | copy-start | bytes 1572868
  187.9 1.7 copy-start.7
  187.9 1.7 copy-start.15
  192.5 17.8 %all-to-all-start.3 = ((bf16[4,64,1024]{2,1,0:T(8,128)(2,1)}), bf16[4,64,1024]{2,1,0:T(8,128)(2,1)S(1)}, u32[]{:S(2)}, u32[]{:S(2)}) async-start(bf16[4,64,1024]{2,1,0:T(8,128)(2,1)} %reshape.166), calls=%async_computation.3 | async-start | bytes 1048576 | tf_op jit(solution)/shard_map/all_to_all | solution.py:132
Sparse Core Ops, SparseCore 0:
  54.9 61.5 all-gather.6
  118.1 65.9 all-gather.4
where the time goes:
time: 220 us; the launch traced here: 219 us
  waiting for transfers between devices  87.7 us (40%)
  blocking collectives  48.5 us (22%)
  local copies, waits for them, and re-layouts  21.6 us (10%)
  starting transfers between devices  19.6 us (9%)
  matrix products  14.6 us (7%)
  between operations  14.5 us (7%)
  other arithmetic  12.3 us (6%)
    all_to_all x1, blocking collectives, per_device(): lax.all_to_all(pack(keys), 'seq', split_axis=0, concat_axis=0, tiled=True)  27.9 us
    all_to_all x1, waiting for transfers between devices, per_device(): lax.all_to_all(pack(values), 'seq', split_axis=0, concat_axis=0, tiled=True)  25.5 us
    all_to_all x1, waiting for transfers between devices, per_device(): lax.all_to_all(to_slots(out_v), 'seq', split_axis=0, concat_axis=0, tiled...  21.8 us
    all_to_all x1, blocking collectives, per_device(): lax.all_to_all(pack(grad_output), 'seq', split_axis=0, concat_axis=0, til...  20.6 us
    all_gather x2, waiting for transfers between devices, entering(): pieces = lax.all_gather(value, axis)  17.4 us
    all_to_all x1, waiting for transfers between devices, per_device(): lax.all_to_all(pack(queries), 'seq', split_axis=0, concat_axis=0, tiled=T...  13.1 us
    all_to_all x1, waiting for transfers between devices, per_device(): lax.all_to_all(to_slots(out_q), 'seq', split_axis=0, concat_axis=0, tiled...  9.87 us
    select_n x6, other arithmetic, hop(): return jnp.where(position < mine, longer, total)  7.5 us
  transfers between devices with their start and end apart: 7, of which 5 were waited for; matrix products, arithmetic and copies ran while one was open for 16% of the time, Pallas kernels for 0%

commit v1 on v0

--- a/solution.py
+++ b/solution.py
@@ -6,6 +6,18 @@
 
 DH = 128
 highest = lax.Precision.HIGHEST
+
+
+def search_lots_all_here(view, where_dim, m):
+    heard = view.shape
+    side_arr = view.reshape(*heard[:where_dim], m, heard[where_dim] // m, *heard[where_dim + 1 :])
+    return jnp.moveaxis(side_arr, where_dim, 0)
+
+
+def _pass_corner(base_x, dim_at):
+    base_x = jnp.moveaxis(base_x, 0, dim_at)
+    z1 = base_x.shape
+    return base_x.reshape(*z1[:dim_at], z1[dim_at] * z1[dim_at + 1], *z1[dim_at + 2 :])
 
 
 def entering(value, axis, join, neutral, backward):
@@ -28,6 +40,23 @@
 
 
 def per_device(queries, keys, values, grad_output, counts):
+
+    def _store_seats_all(in_array, dev_axis, my_data, shard_in=0):
+        carry = lax.axis_size(dev_axis)
+        v_now = lax.axis_index(dev_axis)
+        built, s_next = (carry, v_now)
+        block_now = search_lots_all_here(in_array, my_data, built)
+        small = block_now
+        for q in range(1, built):
+            reply, value_now = ((s_next + q) % built, (s_next - q) % built)
+            new = lax.dynamic_index_in_dim(block_now, reply, 0)
+            pieces_in = []
+            for j in range(built):
+                pieces_in.append((j, (j + q) % built))
+            finding = lax.ppermute(new, axis_name=dev_axis, perm=pieces_in)
+            small = lax.dynamic_update_slice_in_dim(small, finding, value_now, axis=0)
+        return _pass_corner(small, shard_in)
+
     shard_count = lax.axis_size("seq")
     local_rows = queries.shape[1]
     width = queries.shape[2]
@@ -131,7 +160,7 @@
     back_q, back_k, back_v = (
         lax.all_to_all(to_slots(out_q), "seq", split_axis=0, concat_axis=0, tiled=True),
         lax.all_to_all(to_slots(out_k), "seq", split_axis=0, concat_axis=0, tiled=True),
-        lax.all_to_all(to_slots(out_v), "seq", split_axis=0, concat_axis=0, tiled=True),
+        _store_seats_all(to_slots(out_v), "seq", 0),
     )
     positions = jnp.arange(local_rows, dtype=jnp.int32)
     member = (

time: 220 us -> 223 us (1.014)
  waiting for transfers between devices: 87.7 us -> 84.5 us
  local copies, waits for them, and re-layouts: 21.6 us -> 24.2 us
    all_to_all x1 -> x0, waiting for transfers between devices: 21.8 us -> none  [per_device(): lax.all_to_all(to_slots(out_v), 'seq', split_axis=0, concat_axis=0, tiled...]
    ppermute x0 -> x3, waiting for transfers between devices: none -> 15.9 us  [_store_seats_all(): finding = lax.ppermute(new, axis_name=dev_axis, perm=pieces_in)]
    all_gather x2, waiting for transfers between devices: 17.4 us -> 30 us  [entering(): pieces = lax.all_gather(value, axis)]
    all_to_all x1, waiting for transfers between devices: 9.87 us -> 0.01 us  [per_device(): lax.all_to_all(to_slots(out_q), 'seq', split_axis=0, concat_axis=0, tiled...]
    ppermute x0 -> x3, starting transfers between devices: none -> 4.51 us  [_store_seats_all(): finding = lax.ppermute(new, axis_name=dev_axis, perm=pieces_in)]
    all_to_all x1 -> x0, starting transfers between devices: 4.14 us -> none  [per_device(): lax.all_to_all(to_slots(out_v), 'seq', split_axis=0, concat_axis=0, tiled...]
  transfers between devices with their start and end apart: 7 -> 9, of which waited for: 5 -> 4; matrix products, arithmetic and copies ran while one was open for 16% -> 19% of each run, Pallas kernels for 0% -> 0%
where the time goes in v1:
time: 223 us; the launch traced here: 222 us
  waiting for transfers between devices  84.5 us (38%)
  blocking collectives  48.5 us (22%)
  local copies, waits for them, and re-layouts  24.2 us (11%)
  starting transfers between devices  20.7 us (9%)
  matrix products  16.5 us (7%)
  between operations  14.5 us (7%)
  other arithmetic  13 us (6%)
    all_gather x2, waiting for transfers between devices, entering(): pieces = lax.all_gather(value, axis)  30 us
    all_to_all x1, blocking collectives, per_device(): lax.all_to_all(pack(keys), 'seq', split_axis=0, concat_axis=0, tiled=True)  27.9 us
    all_to_all x1, waiting for transfers between devices, per_device(): lax.all_to_all(pack(values), 'seq', split_axis=0, concat_axis=0, tiled=True)  25.5 us
    all_to_all x1, blocking collectives, per_device(): lax.all_to_all(pack(grad_output), 'seq', split_axis=0, concat_axis=0, til...  20.6 us
    ppermute x3, waiting for transfers between devices, _store_seats_all(): finding = lax.ppermute(new, axis_name=dev_axis, perm=pieces_in)  15.9 us
    all_to_all x1, waiting for transfers between devices, per_device(): lax.all_to_all(pack(queries), 'seq', split_axis=0, concat_axis=0, tiled=T...  13.1 us
    select_n x6, other arithmetic, hop(): return jnp.where(position < mine, longer, total)  7.47 us
    all_to_all x1, starting transfers between devices, per_device(): lax.all_to_all(to_slots(out_k), 'seq', split_axis=0, concat_axis=0, tiled...  5.07 us
  transfers between devices with their start and end apart: 9, of which 4 were waited for; matrix products, arithmetic and copies ran while one was open for 19% of the time, Pallas kernels for 0%

profile of v1, /device:TPU:0, one launch (start us, length us, event | category | flops | bytes accessed | tf_op | source)
XLA Modules:
  0.0 222.0 jit_solution(5695558334169814718)
XLA Ops:
  15.8 20.6 %all_to_all.30 = bf16[4,64,1024]{2,1,0:T(8,128)(2,1)S(1)} all-to-all(bf16[4,64,1024]{2,1,0:T(8,128)(2,1)S(1)} %bitcast.72), channel_id=1, replica_groups=mesh['groups'=2,'seq'=4,'dp'=2,'mp'=2] {'seq'}, dimensions={0} | all-to-all | bytes 1048576 | tf_op jit(solution)/shard_map/all_to_all | solution.py:90
  36.4 3.5 %all-to-all-start.4 = ((bf16[4,64,1024]{2,1,0:T(8,128)(2,1)}), bf16[4,64,1024]{2,1,0:T(8,128)(2,1)S(1)}, u32[]{:S(2)}, u32[]{:S(2)}) async-start(bf16[4,64,1024]{2,1,0:T(8,128)(2,1)} %bitcast.14), calls=%async_computation.4 | async-start | bytes 1048576 | tf_op jit(solution)/shard_map/all_to_all | solution.py:87
  40.3 13.1 %all-to-all-done.4 = bf16[4,64,1024]{2,1,0:T(8,128)(2,1)S(1)} async-done(((bf16[4,64,1024]{2,1,0:T(8,128)(2,1)}), bf16[4,64,1024]{2,1,0:T(8,128)(2,1)S(1)}, u32[]{:S(2)}, u32[]{:S(2)}) %all-to-all-start.4) | async-done | bytes 524320 | tf_op jit(solution)/shard_map/all_to_all | solution.py:87
  54.7 27.9 %all_to_all.31 = bf16[4,64,1024]{2,1,0:T(8,128)(2,1)S(1)} all-to-all(bf16[4,64,1024]{2,1,0:T(8,128)(2,1)S(1)} %bitcast.71), channel_id=1, replica_groups=mesh['groups'=2,'seq'=4,'dp'=2,'mp'=2] {'seq'}, dimensions={0} | all-to-all | bytes 1048576 | tf_op jit(solution)/shard_map/all_to_all | solution.py:88
  82.7 4.1 %all-to-all-start.1 = ((bf16[4,64,1024]{2,1,0:T(8,128)(2,1)}), bf16[4,64,1024]{2,1,0:T(8,128)(2,1)S(1)}, u32[]{:S(2)}, u32[]{:S(2)}) async-start(bf16[4,64,1024]{2,1,0:T(8,128)(2,1)} %bitcast.6), calls=%async_computation.1 | async-start | bytes 1048576 | tf_op jit(solution)/shard_map/all_to_all | solution.py:89
  86.9 25.5 %all-to-all-done.1 = bf16[4,64,1024]{2,1,0:T(8,128)(2,1)S(1)} async-done(((bf16[4,64,1024]{2,1,0:T(8,128)(2,1)}), bf16[4,64,1024]{2,1,0:T(8,128)(2,1)S(1)}, u32[]{:S(2)}, u32[]{:S(2)}) %all-to-all-start.1) | async-done | bytes 524320 | tf_op jit(solution)/shard_map/all_to_all | solution.py:89
  115.3 1.8 fusion.49
  117.1 1.5 fusion.53
  118.7 3.2 %rev.3 = f32[4,8,128,128]{3,2,1,0:T(8,128)} reverse(f32[4,8,128,128]{3,2,1,0:T(8,128)} %bitcast.73), dimensions={0} | reverse | bytes 4194304 | tf_op jit(solution)/shard_map/rev | solution.py:27
  121.9 3.8 %while.35 = (s32[]{:T(128)}, f32[8,128,128]{2,1,0:T(8,128)S(1)}, s32[]{:T(128)}, f32[4,8,128,128]{3,2,1,0:T(8,128)}, s32[]{:T(128)}, /*index=5*/s32[]{:T(128)}) while((s32[]{:T(128)}, f32[8,128,128]{2,1,0:T(8,128)S(1)}, s32[]{:T(128)}, f32[4,8,128,128]{3,2,1,0:T(8,128)}, s32[]{:T(128)}, /*index=5*/s32[]{:T(128)}) %tuple.77), condition=%wide.region_6.9_spmd.clone, body=%wide.region_5.8_spmd.clone.sunk | while | flops 393220 | bytes 1572965 | solution.py:35
  125.7 2.0 fusion.60
  127.8 2.8 %fusion.39 = bf16[256,8,128]{0,2,1:T(8,128)(2,1)} fusion(f32[8,128,256]{2,1,0:T(8,128)S(1)} %fusion.60, bf16[256,8,128]{0,2,1:T(8,128)(2,1)S(1)} %copy-done.6, f32[8,256,256]{2,1,0:T(8,128)S(1)} %copy-done.14, f32[256,256]{1,0:T(8,128)} %fusion.62), kind=kOutput, calls=%fused_computation.26 | convolution fusion | flops 806617088 | bytes 4456448 | tf_op jit(solution)/shard_map/while/body/eval_jaxpr/hrs,rhb->shb/dot_general | solution.py:144
  130.6 2.1 copy.67
  132.7 2.1 reshape_reshape.4
  135.8 1.8 fusion.51
  139.9 2.1 reshape.164
  142.0 5.1 %all-to-all-start.5 = ((bf16[4,64,1024]{2,1,0:T(8,128)(2,1)}), bf16[4,64,1024]{2,1,0:T(8,128)(2,1)}, u32[]{:S(2)}, u32[]{:S(2)}) async-start(bf16[4,64,1024]{2,1,0:T(8,128)(2,1)} %reshape.164), calls=%async_computation.5 | async-start | bytes 1048576 | tf_op jit(solution)/shard_map/all_to_all | solution.py:162
  147.0 30.0 %all-gather.5.cloned.1.call-done = f32[32,128,128]{2,1,0:T(8,128)} async-done(((f32[8,128,128]{2,1,0:T(8,128)}), f32[32,128,128]{2,1,0:T(8,128)}) %all-gather.5.cloned.1.call-update) | async-done | bytes 2097168 | tf_op jit(solution)/shard_map/all_gather | solution.py:25
  177.0 3.8 %while.34 = (s32[]{:T(128)}, f32[8,128,128]{2,1,0:T(8,128)S(1)}, s32[]{:T(128)}, f32[4,8,128,128]{3,2,1,0:T(8,128)}, s32[]{:T(128)}, /*index=5*/s32[]{:T(128)}) while((s32[]{:T(128)}, f32[8,128,128]{2,1,0:T(8,128)S(1)}, s32[]{:T(128)}, f32[4,8,128,128]{3,2,1,0:T(8,128)}, s32[]{:T(128)}, /*index=5*/s32[]{:T(128)}) %tuple.87), condition=%wide.region_2.4_spmd.clone, body=%wide.region_1.3_spmd.clone.sunk | while | flops 393220 | bytes 1572965 | solution.py:35
  180.8 1.7 fusion.45
  185.3 3.5 %all-to-all-start.3 = ((bf16[4,64,1024]{2,1,0:T(8,128)(2,1)}), bf16[4,64,1024]{2,1,0:T(8,128)(2,1)S(1)}, u32[]{:S(2)}, u32[]{:S(2)}) async-start(bf16[4,64,1024]{2,1,0:T(8,128)(2,1)} %reshape.160), calls=%async_computation.3 | async-start | bytes 1048576 | tf_op jit(solution)/shard_map/all_to_all | solution.py:161
  189.9 3.0 %collective-permute-start.1 = (bf16[1,1,64,1024]{3,2,0,1:T(8,128)(2,1)S(1)}, bf16[1,1,64,1024]{3,2,0,1:T(8,128)(2,1)S(1)}, u32[]{:S(2)}, u32[]{:S(2)}) collective-permute-start(bf16[1,1,64,1024]{3,2,0,1:T(8,128)(2,1)S(1)} %get-tuple-element.251), channel_id=1, source_target_pairs={{0,8},{4,12},{8,0},{12,4},{1,9},{5,13},{9,1},{13,5},{2,10},{6,14},... | collective-permute-start | bytes 393224 | tf_op jit(solution)/shard_map/ppermute | solution.py:56
  194.3 15.8 %collective-permute-done.1 = bf16[1,1,64,1024]{3,2,0,1:T(8,128)(2,1)S(1)} collective-permute-done((bf16[1,1,64,1024]{3,2,0,1:T(8,128)(2,1)S(1)}, bf16[1,1,64,1024]{3,2,0,1:T(8,128)(2,1)S(1)}, u32[]{:S(2)}, u32[]{:S(2)}) %collective-permute-start.1) | collective-permute-done | bytes 131104 | tf_op jit(solution)/shard_map/ppermute | solution.py:56
  211.1 2.2 gather_fusion.5
  (89 shorter events, 32.1 us)
Async XLA Ops:
  7.2 2.5 %copy-start = (bf16[1,128,1024]{2,1,0:T(8,128)(2,1)S(1)}, bf16[1,128,1024]{2,1,0:T(8,128)(2,1)}, u32[]{:S(2)}) copy-start(bf16[1,128,1024]{2,1,0:T(8,128)(2,1)} %param.13) | copy-start | bytes 786436
  9.7 1.2 copy-start.1
  10.9 1.2 copy-start.2
  36.4 17.1 %all-to-all-start.4 = ((bf16[4,64,1024]{2,1,0:T(8,128)(2,1)}), bf16[4,64,1024]{2,1,0:T(8,128)(2,1)S(1)}, u32[]{:S(2)}, u32[]{:S(2)}) async-start(bf16[4,64,1024]{2,1,0:T(8,128)(2,1)} %bitcast.14), calls=%async_computation.4 | async-start | bytes 1048576 | tf_op jit(solution)/shard_map/all_to_all | solution.py:87
  39.8 78.8 %all-gather.7.cloned.1.call-start = ((), (), s32[]{:S(2)}) async-start(), calls=%async_computation.7 | async-start | bytes 2621440 | tf_op jit(solution)/shard_map/all_gather | solution.py:25
  40.3 42.3 %copy-start.5 = (bf16[256,8,128]{0,2,1:T(8,128)(2,1)}, bf16[256,8,128]{0,2,1:T(8,128)(2,1)S(1)}, u32[]{:S(2)}) copy-start(bf16[256,8,128]{0,2,1:T(8,128)(2,1)S(1)} %copy.66) | copy-start | bytes 1572868
  53.5 61.7 %copy-start.10 = (bf16[32,8,8,128]{3,2,1,0:T(8,128)(2,1)}, bf16[32,8,8,128]{3,2,1,0:T(8,128)(2,1)S(1)}, u32[]{:S(2)}) copy-start(bf16[32,8,8,128]{3,2,1,0:T(8,128)(2,1)S(1)} %copy.72) | copy-start | bytes 1572868
  82.7 29.7 %all-to-all-start.1 = ((bf16[4,64,1024]{2,1,0:T(8,128)(2,1)}), bf16[4,64,1024]{2,1,0:T(8,128)(2,1)S(1)}, u32[]{:S(2)}, u32[]{:S(2)}) async-start(bf16[4,64,1024]{2,1,0:T(8,128)(2,1)} %bitcast.6), calls=%async_computation.1 | async-start | bytes 1048576 | tf_op jit(solution)/shard_map/all_to_all | solution.py:89
  86.8 90.2 %all-gather.5.cloned.1.call-start = ((), (), s32[]{:S(2)}) async-start(), calls=%async_computation.6 | async-start | bytes 2621440 | tf_op jit(solution)/shard_map/all_gather | solution.py:25
  86.9 28.4 %copy-start.8 = (bf16[32,8,8,128]{3,2,1,0:T(8,128)(2,1)}, bf16[32,8,8,128]{3,2,1,0:T(8,128)(2,1)S(1)}, u32[]{:S(2)}) copy-start(bf16[32,8,8,128]{3,2,1,0:T(8,128)(2,1)S(1)} %copy.69) | copy-start | bytes 1572868
  114.5 2.6 %copy-start.13 = (bf16[32,8,8,128]{3,2,1,0:T(8,128)(2,1)S(1)}, bf16[32,8,8,128]{3,2,1,0:T(8,128)(2,1)}, u32[]{:S(2)}) copy-start(bf16[32,8,8,128]{3,2,1,0:T(8,128)(2,1)} %copy-done.12) | copy-start | bytes 1572868
  125.7 2.0 copy-start.6
  125.7 2.1 copy-start.14
  134.8 2.9 %copy-start.11 = (bf16[32,8,8,128]{3,2,1,0:T(8,128)(2,1)S(1)}, bf16[32,8,8,128]{3,2,1,0:T(8,128)(2,1)}, u32[]{:S(2)}) copy-start(bf16[32,8,8,128]{3,2,1,0:T(8,128)(2,1)} %copy-done.10) | copy-start | bytes 1572868
  134.8 2.9 %copy-start.15 = (f32[256,256]{1,0:T(8,128)S(1)}, f32[256,256]{1,0:T(8,128)}, u32[]{:S(2)}) copy-start(f32[256,256]{1,0:T(8,128)} %fusion.62) | copy-start | bytes 786436
  135.8 53.2 %collective-permute-start = (bf16[1,1,64,1024]{3,2,0,1:T(8,128)(2,1)S(1)}, bf16[1,1,64,1024]{3,2,0,1:T(8,128)(2,1)}, u32[]{:S(2)}, u32[]{:S(2)}) collective-permute-start(bf16[1,1,64,1024]{3,2,0,1:T(8,128)(2,1)S(1)} %constant_dynamic-slice_fusion.2), channel_id=1, source_target_pairs={{0,4},{4,8},{8,12},{12,0},{1,5},{5,9},{9,13},{13,1},{2,6},{6,10},{... | collective-permute-start | bytes 393224 | tf_op jit(solution)/shard_map/ppermute | solution.py:56
  142.0 43.4 %all-to-all-start.5 = ((bf16[4,64,1024]{2,1,0:T(8,128)(2,1)}), bf16[4,64,1024]{2,1,0:T(8,128)(2,1)}, u32[]{:S(2)}, u32[]{:S(2)}) async-start(bf16[4,64,1024]{2,1,0:T(8,128)(2,1)} %reshape.164), calls=%async_computation.5 | async-start | bytes 1048576 | tf_op jit(solution)/shard_map/all_to_all | solution.py:162
  177.0 3.8 %copy-start.7 = (bf16[256,8,128]{0,2,1:T(8,128)(2,1)S(1)}, bf16[256,8,128]{0,2,1:T(8,128)(2,1)}, u32[]{:S(2)}) copy-start(bf16[256,8,128]{0,2,1:T(8,128)(2,1)} %copy-done.5) | copy-start | bytes 1572868
  180.8 1.7 copy-start.9
  180.8 1.7 copy-start.16
  184.0 4.9 %copy-start.4 = (bf16[4,1,64,1024]{3,2,0,1:T(8,128)(2,1)S(1)}, bf16[4,1,64,1024]{3,2,0,1:T(8,128)(2,1)}, u32[]{:S(2)}) copy-start(bf16[4,1,64,1024]{3,2,0,1:T(8,128)(2,1)} %reshape_reshape.4) | copy-start | bytes 1572868
  185.3 27.9 %all-to-all-start.3 = ((bf16[4,64,1024]{2,1,0:T(8,128)(2,1)}), bf16[4,64,1024]{2,1,0:T(8,128)(2,1)S(1)}, u32[]{:S(2)}, u32[]{:S(2)}) async-start(bf16[4,64,1024]{2,1,0:T(8,128)(2,1)} %reshape.160), calls=%async_computation.3 | async-start | bytes 1048576 | tf_op jit(solution)/shard_map/all_to_all | solution.py:161
  189.9 20.3 %collective-permute-start.1 = (bf16[1,1,64,1024]{3,2,0,1:T(8,128)(2,1)S(1)}, bf16[1,1,64,1024]{3,2,0,1:T(8,128)(2,1)S(1)}, u32[]{:S(2)}, u32[]{:S(2)}) collective-permute-start(bf16[1,1,64,1024]{3,2,0,1:T(8,128)(2,1)S(1)} %get-tuple-element.251), channel_id=1, source_target_pairs={{0,8},{4,12},{8,0},{12,4},{1,9},{5,13},{9,1},{13,5},{2,10},{6,14},... | collective-permute-start | bytes 393224 | tf_op jit(solution)/shard_map/ppermute | solution.py:56
  192.8 17.4 %collective-permute-start.2 = (bf16[1,1,64,1024]{3,2,0,1:T(8,128)(2,1)S(1)}, bf16[1,1,64,1024]{3,2,0,1:T(8,128)(2,1)S(1)}, u32[]{:S(2)}, u32[]{:S(2)}) collective-permute-start(bf16[1,1,64,1024]{3,2,0,1:T(8,128)(2,1)S(1)} %get-tuple-element.250), channel_id=1, source_target_pairs={{0,12},{4,0},{8,4},{12,8},{1,13},{5,1},{9,5},{13,9},{2,14},{6,2},{... | collective-permute-start | bytes 393224 | tf_op jit(solution)/shard_map/ppermute | solution.py:56
  (2 other events, 2.0 us)
Sparse Core Ops, SparseCore 0:
  54.9 61.5 all-gather.6
  118.0 58.9 all-gather.4
